TPU v7x, 256 devices: a whole 4x4x8 slice. The times are simulated.
256 devices in a mesh: snap: 16 (over z, y_lo), space: 16 (over x, y_hi, core).
Axes of the slice: x: 4, y: 4 (y_hi: 2, y_lo: 2; y = y_hi * 2 + y_lo), z: 8, core: 2. Of those that a mesh axis runs over, the one named last changes fastest.
Arguments:
- snapshots: bfloat16 [2048, 2, 64, 720], P('snap', None, 'space'), may hold values from -6 to 6
- lon_coeff: float32 [2, 64, 720], P(None, 'space'), may hold values from 0.05 to 0.24
- lat_coeff: float32 [2, 64, 720], P(None, 'space'), may hold values from 0.1 to 0.24
Outputs:
- gram: float32 [2048, 2048], P('snap', 'space')
All inputs are finite; a program needn't handle non-finite values.
Results may differ from a plain program's by a relative error of at most 0.00062.
Values may be sent and summed in bfloat16 or wider, within the bound.
A program may use at most 128 MiB of HBM per device.

v0:
```python
import math

import jax
import jax.numpy as jnp
from jax import lax
from jax.sharding import PartitionSpec as P


def padded_2(cells, sides, width):
    for axis, dim in sides:
        count = lax.axis_size(axis)
        ends = count - 1
        head = lax.slice_in_dim(cells, 0, width, axis=dim)
        tail = lax.slice_in_dim(cells, cells.shape[dim] - width, cells.shape[dim], axis=dim)
        cells = jnp.concatenate(
            [
                lax.ppermute(tail, axis, [(i, (i + 1) % count) for i in range(ends)]),
                cells,
                lax.ppermute(head, axis, [((i + 1) % count, i) for i in range(ends)]),
            ],
            axis=dim,
        )
    return cells


def inner_tile(left, right):
    return lax.dot_general(
        left, right, (((1,), (1,)), ((), ())), preferred_element_type=jnp.float32
    )


def shards(snapshots, lon_coeff, lat_coeff):
    snap_rows, fields, rows, nlon = snapshots.shape
    bands = lax.axis_size("space")
    padded = padded_2(snapshots, (("space", 2),), 1).astype(jnp.float32)
    values = snapshots.astype(jnp.float32)
    lon_part = jnp.roll(values, 1, axis=3) + jnp.roll(values, -1, axis=3) - 2.0 * values
    lat_part = padded[:, :, 2:] + padded[:, :, :-2] - 2.0 * values
    smooth = values + lon_coeff * lon_part + lat_coeff * lat_part
    nlat = bands * rows
    every_row = jnp.arange(nlat).astype(jnp.float32)
    every_cos = jnp.cos((45.0 + 0.5 * (every_row + 0.5 - nlat / 2.0)) * (math.pi / 180.0))
    total = fields * nlon * jnp.sum(every_cos)
    my_rows = (lax.axis_index("space") * rows + jnp.arange(rows)).astype(jnp.float32)
    cosine = jnp.cos((45.0 + 0.5 * (my_rows + 0.5 - nlat / 2.0)) * (math.pi / 180.0))
    factor = jnp.sqrt(cosine) * total ** (-0.25)
    scaled = (smooth * factor[:, None]).astype(jnp.bfloat16).reshape(snap_rows, -1)
    partial_value = inner_tile(scaled, lax.all_gather(scaled, "snap", axis=0, tiled=True))
    return lax.psum_scatter(partial_value, "space", scatter_dimension=1, tiled=True)


def solution(mesh):
    return jax.shard_map(
        shards,
        mesh=mesh,
        in_specs=(P("snap", None, "space", None), P(None, "space", None), P(None, "space", None)),
        out_specs=P("snap", "space"),
        check_vma=False,
    )
```

profile of v0, /device:TPU:33, one launch (start us, length us, event | category | flops | bytes accessed | tf_op | source)
XLA Modules:
  0.0 611.9 jit_solution(12110628258936550416)
XLA Ops:
  6.5 0.0 copy-start
  6.5 0.0 all-gather.2.cloned.1.call-start
  6.5 1.3 fusion.10
  7.8 5.4 collective-permute-start
  13.2 1.9 collective-permute-start.1
  15.1 0.6 cosine_reduce_fusion
  15.8 0.7 fusion.9
  17.2 0.1 sqrt_multiply_fusion
  17.3 0.0 copy-done
  17.3 0.4 fusion.8
  17.7 0.0 copy-start.1
  17.7 0.0 copy-start.2
  17.7 0.0 collective-permute-done
  17.7 5.8 collective-permute-done.1
  23.5 0.3 maximum_convert_fusion
  23.9 0.0 copy-done.1
  23.9 0.0 copy-done.2
  23.9 3.9 fusion.4
  27.8 0.0 all-gather.2.cloned.1.call-update
  27.8 0.0 reduce-scatter.2.cloned.1.call-start
  27.9 490.0 %all-gather.2.cloned.1.call-done = bf16[2048,5760]{0,1:T(8,128)(2,1)} async-done(((bf16[128,5760]{0,1:T(8,128)(2,1)}), bf16[2048,5760]{0,1:T(8,128)(2,1)}) %all-gather.2.cloned.1.call-update) | async-done | bytes 23592976 | tf_op jit(solution)/shard_map/all_gather | solution.py:48
  517.8 12.5 %fusion.11 = f32[128,2048]{1,0:T(8,128)} fusion(bf16[128,5760]{0,1:T(8,128)(2,1)} %bitcast.4, bf16[2048,5760]{0,1:T(8,128)(2,1)} %all-gather.2.cloned.1.call-done), kind=kOutput, calls=%fused_computation.16 | convolution fusion | flops 3019898880 | bytes 26116096 | tf_op jit(solution)/shard_map/dot_general | solution.py:27
  530.4 0.0 reduce-scatter.2.cloned.1.call-update
  530.4 74.6 %reduce-scatter.2.cloned.1.call-done = f32[128,128]{1,0:T(8,128)} async-done(((f32[128,2048]{1,0:T(8,128)}), f32[128,128]{1,0:T(8,128)}) %reduce-scatter.2.cloned.1.call-update) | async-done | bytes 65552 | tf_op jit(solution)/shard_map/reduce_scatter | solution.py:49
Async XLA Ops:
  6.5 10.7 %copy-start = (bf16[128,2,4,720]{0,3,2,1:T(8,128)(2,1)S(1)}, bf16[128,2,4,720]{0,3,2,1:T(8,128)(2,1)}, u32[]{:S(2)}) copy-start(bf16[128,2,4,720]{0,3,2,1:T(8,128)(2,1)} %param.3) | copy-start | bytes 4423684
  6.5 511.3 %all-gather.2.cloned.1.call-start = ((), (), s32[]{:S(2)}) async-start(), calls=%async_computation.1 | async-start | bytes 25067520 | tf_op jit(solution)/shard_map/all_gather | solution.py:48
  7.8 9.9 %collective-permute-start = (bf16[128,2,1,720]{0,3,2,1:T(8,128)(2,1)S(1)}, bf16[128,2,1,720]{0,3,2,1:T(8,128)(2,1)S(1)}, u32[]{:S(2)}, u32[]{:S(2)}) collective-permute-start(bf16[128,2,1,720]{0,3,2,1:T(8,128)(2,1)S(1)} %get-tuple-element.9), channel_id=1, source_target_pairs={{0,1},{1,2},{2,3},{3,4},{4,5},{5,6},{6,7},{7,8},{8,9},{9,10},{10,1... | collective-permute-start | bytes 1105928 | tf_op jit(solution)/shard_map/ppermute | solution.py:17
  13.2 10.3 %collective-permute-start.1 = (bf16[128,2,1,720]{0,3,2,1:T(8,128)(2,1)S(1)}, bf16[128,2,1,720]{0,3,2,1:T(8,128)(2,1)S(1)}, u32[]{:S(2)}, u32[]{:S(2)}) collective-permute-start(bf16[128,2,1,720]{0,3,2,1:T(8,128)(2,1)S(1)} %get-tuple-element.10), channel_id=1, source_target_pairs={{1,0},{2,1},{3,2},{4,3},{5,4},{6,5},{7,6},{8,7},{9,8},{10,9},{11,1... | collective-permute-start | bytes 1105928 | tf_op jit(solution)/shard_map/ppermute | solution.py:19
  17.7 6.2 %copy-start.1 = (f32[2,4,720]{2,1,0:T(4,128)S(1)}, f32[2,4,720]{2,1,0:T(4,128)}, u32[]{:S(2)}) copy-start(f32[2,4,720]{2,1,0:T(4,128)} %param.5) | copy-start | bytes 69124
  17.7 6.2 %copy-start.2 = (f32[2,4,720]{2,1,0:T(4,128)S(1)}, f32[2,4,720]{2,1,0:T(4,128)}, u32[]{:S(2)}) copy-start(f32[2,4,720]{2,1,0:T(4,128)} %param.4) | copy-start | bytes 69124
  27.8 577.2 %reduce-scatter.2.cloned.1.call-start = ((), (), s32[]{:S(2)}) async-start(), calls=%async_computation.2 | async-start | bytes 1114112 | tf_op jit(solution)/shard_map/reduce_scatter | solution.py:49
Sparse Core Ops, SparseCore 0:
  27.9 489.8 all-gather.1
  530.5 74.4 reduce-scatter.1
where the time goes:
time: 614 us; the launch traced here: 612 us
  waiting for transfers between devices  570 us (93%)
  between operations  14.2 us (2%)
  matrix products  12.5 us (2%)
  starting transfers between devices  7.35 us (1%)
    all_gather x1, waiting for transfers between devices, shards(): lax.all_gather(scaled, 'snap', axis=0, tiled=True)  490 us
    reduce_scatter x1, waiting for transfers between devices, shards(): lax.psum_scatter(partial_value, 'space', scatter_dimension=1, tiled=True)  74.6 us
    dot_general x1, matrix products, inner_tile(): lax.dot_general(left, right, (((1,), (1,)), ((), ())), preferred_element_...  12.5 us
  transfers between devices with their start and end apart: 4, of which 3 were waited for; matrix products, arithmetic and copies ran while one was open for 0% of the time, Pallas kernels for 0%

commit v1 on v0

v1 whole, which is shorter than its diff:
```python
import functools
import math

import jax
import jax.numpy as jnp
import numpy as np
from jax import lax
from jax.experimental import pallas as pl
from jax.experimental.pallas import tpu as pltpu
from jax.sharding import PartitionSpec as P

MESH = pl.DeviceIdType.MESH
NLON = 720
KPAD = 1536
B = 128
CH = 144


def row_factors(fields, nlat, nlon):
    lat = (45.0 + 0.5 * (np.arange(nlat) + 0.5 - nlat / 2.0)) * (math.pi / 180.0)
    cosine = np.cos(lat)
    total = fields * nlon * cosine.sum()
    return (np.sqrt(cosine) * total ** (-0.25)).astype(np.float32)


def kernel(x_ref, coef_ref, fac_ref, o_ref,
           halo, v32, sc, rows, a2, part, xin, q, yin, fin, zin, mout, minb,
           halo_s, halo_r, loc_s, z_s, z_r, y_s, y_r, c_s, c_r, x_s, x_r, h_s, h_r, f_s, f_r, m_s, m_r):
    snap = lax.axis_index("snap")
    space = lax.axis_index("space")
    z, yl = snap // 2, snap % 2
    xx, yh, core = space // 4, (space // 2) % 2, space % 2
    m_me = space // 2
    same = (core == yl).astype(jnp.int32)
    nb = 4 + same
    kk0 = 1 - same
    off = jnp.where(same == 1, 0, yl)

    def copy(src, dst, ss, rs, dev):
        return pltpu.make_async_remote_copy(
            src_ref=src, dst_ref=dst, send_sem=ss, recv_sem=rs, device_id=dev, device_id_type=MESH)

    up_dev = (snap, jnp.maximum(space - 1, 0))
    dn_dev = (snap, jnp.minimum(space + 1, 15))
    y_dev = (z * 2 + 1 - yl, space)
    c_dev = (snap, m_me * 2 + 1 - core)
    h_dev = (snap, xx * 4 + (1 - yh) * 2 + core)
    m_dev = (space, snap)

    barrier = pltpu.get_barrier_semaphore()

    def greet(dev):
        pl.semaphore_signal(barrier, inc=1, device_id=dev, device_id_type=MESH)

    for dz in range(1, 8):
        greet((((z + dz) % 8) * 2 + yl, space))
    for dx in range(1, 4):
        greet((snap, ((xx + dx) % 4) * 4 + yh * 2 + core))
    greet(y_dev)
    greet(c_dev)
    greet(h_dev)

    @pl.when(space > 0)
    def _():
        greet(up_dev)

    @pl.when(space < 15)
    def _():
        greet(dn_dev)

    @pl.when(snap != space)
    def _():
        greet(m_dev)

    pl.semaphore_wait(
        barrier,
        13 + (space > 0).astype(jnp.int32) + (space < 15).astype(jnp.int32) + (snap != space).astype(jnp.int32))

    def halo_down(f):
        return copy(x_ref.at[4 * f + 3], halo.at[0, f], halo_s.at[0, f], halo_r.at[0, f], dn_dev)

    def halo_up(f):
        return copy(x_ref.at[4 * f], halo.at[1, f], halo_s.at[1, f], halo_r.at[1, f], up_dev)

    @pl.when(space < 15)
    def _():
        for f in range(2):
            halo_down(f).start()

    @pl.when(space > 0)
    def _():
        for f in range(2):
            halo_up(f).start()

    @pl.when(space == 0)
    def _():
        halo[0] = jnp.zeros((2, NLON, B), jnp.bfloat16)

    @pl.when(space == 15)
    def _():
        halo[1] = jnp.zeros((2, NLON, B), jnp.bfloat16)

    def slot(yy, zz, cc):
        return rows.at[yy, zz, pl.ds(pl.multiple_of(cc * NLON, 16), NLON), :]

    def stencil(j):
        f, row = divmod(j, 4)
        v = x_ref[j].astype(jnp.float32)
        v32[j, pl.ds(8, NLON), :] = v
        v32[j, 7:8, :] = v[NLON - 1:, :]
        v32[j, NLON + 8:NLON + 9, :] = v[:1, :]
        scale = fac_ref[space * 4 + row]
        for s in range(0, NLON, CH):
            a = v32[j, pl.ds(8 + s, CH), :]
            west = v32[j, pl.ds(7 + s, CH), :]
            east = v32[j, pl.ds(9 + s, CH), :]
            if row == 0:
                north = halo[0, f, pl.ds(s, CH), :]
            else:
                north = x_ref[j - 1, pl.ds(s, CH), :]
            if row == 3:
                south = halo[1, f, pl.ds(s, CH), :]
            else:
                south = x_ref[j + 1, pl.ds(s, CH), :]
            lon_part = west + east - 2.0 * a
            lat_part = south.astype(jnp.float32) + north.astype(jnp.float32) - 2.0 * a
            smooth = a + coef_ref[pl.ds(s, CH), j:j + 1] * lon_part + coef_ref[pl.ds(s, CH), 8 + j:9 + j] * lat_part
            sc[j, pl.ds(s, CH), :] = (smooth * scale).astype(jnp.bfloat16)

    def z_copy(j):
        return copy(sc.at[j], slot(yl, z, core), z_s.at[j], z_r.at[z], (j * 2 + yl, space))

    def local_copy(j):
        return pltpu.make_async_copy(sc.at[j], slot(yl, z, core), loc_s)

    def z_start(j):
        @pl.when(z == j)
        def _():
            local_copy(j).start()

        @pl.when(z != j)
        def _():
            z_copy(j).start()

    rows[:, :, 2 * NLON:, :] = jnp.zeros((2, 8, KPAD - 2 * NLON, B), jnp.bfloat16)

    last = None
    for j in (1, 2, 5, 6):
        stencil(j)
        if last is not None:
            z_start(last)
        last = j

    @pl.when(space > 0)
    def _():
        for f in range(2):
            halo_down(f).wait_recv()

    @pl.when(space < 15)
    def _():
        for f in range(2):
            halo_up(f).wait_recv()

    for j in (0, 3, 4, 7):
        stencil(j)
        z_start(last)
        last = j
    z_start(last)

    def near(i):
        return (z + 8 + ((i + 1) // 2) * (2 * (i % 2) - 1)) % 8

    def y_copy(zz):
        return copy(slot(yl, zz, core), slot(yl, zz, core), y_s.at[zz], y_r.at[zz], y_dev)

    def y_arrive(zz):
        copy(slot(1 - yl, zz, core), slot(1 - yl, zz, core), y_s.at[zz], y_r.at[zz], y_dev).wait_recv()

    def c_copy(yy, zz):
        return copy(slot(yy, zz, core), slot(yy, zz, core), c_s.at[yy, zz], c_r.at[yy, zz], c_dev)

    def c_arrive(yy, zz):
        copy(slot(yy, zz, 1 - core), slot(yy, zz, 1 - core), c_s.at[yy, zz], c_r.at[yy, zz], c_dev).wait_recv()

    def turn(zz):
        c_arrive(yl, zz)
        t = rows[yl, zz].T
        a2[pl.ds(pl.multiple_of(zz * B, B), B), :] = t
        a2[pl.ds(pl.multiple_of(zz * B + 8 * B, B), B), :] = t

    def step(i, carry):
        zz = near(i)

        @pl.when(i == 0)
        def _():
            local_copy(0).wait()

        @pl.when(i > 0)
        def _():
            copy(sc.at[0], slot(yl, zz, core), z_s.at[0], z_r.at[zz], (snap, space)).wait_recv()

        y_copy(zz).start()
        c_copy(yl, zz).start()

        @pl.when(i > 0)
        def _():
            before = near(i - 1)
            y_arrive(before)
            c_copy(1 - yl, before).start()
            turn(before)

        return carry

    lax.fori_loop(0, 8, step, 0)
    y_arrive(near(7))
    c_copy(1 - yl, near(7)).start()
    turn(near(7))

    def arrive(zz, carry):
        c_arrive(1 - yl, zz)
        return carry

    lax.fori_loop(0, 8, arrive, 0)

    def blk(kk):
        return pl.ds(pl.multiple_of(kk * B, B), B)

    def x_copy(m, kk):
        return copy(part.at[m, blk(kk), :], xin.at[xx, m % 2, blk(kk), :], x_s.at[m, kk],
                    x_r.at[xx, m % 2, kk], (snap, (m // 2) * 4 + yh * 2 + core))

    def m_of(t):
        return ((xx + t // 2 + 1) % 4) * 2 + t % 2

    def product(t, carry):
        m = m_of(t)
        start = pl.multiple_of(((m + 8 - 4 - off) % 8) * B, B)
        part[m] = jnp.dot(a2[pl.ds(start, 5 * B), :], rows[core, m], preferred_element_type=jnp.float32)

        @pl.when((t > 0) & (t < 7))
        def _():
            def send(kk, c):
                x_copy(m_of(t - 1), kk).start()
                return c

            lax.fori_loop(kk0, 5, send, 0)

        return carry

    lax.fori_loop(0, 8, product, 0)

    def x_sum(yy, kk):
        m = 2 * xx + yy
        total = part[m, blk(kk), :]
        for dx in range(1, 4):
            src = (xx + dx) % 4
            copy(part.at[0, blk(kk), :], xin.at[src, yy, blk(kk), :], x_s.at[m, kk], x_r.at[src, yy, kk],
                 (snap, space)).wait_recv()
            total = total + xin[src, yy, blk(kk), :]
        return total

    def h_copy(kk):
        return copy(q.at[blk(kk), :], yin.at[blk(kk), :], h_s.at[kk], h_r.at[kk], h_dev)

    def other_half(kk, carry):
        q[blk(kk), :] = x_sum(1 - yh, kk)

        @pl.when(kk > kk0)
        def _():
            h_copy(kk - 1).start()

        return carry

    lax.fori_loop(kk0, 5, other_half, 0)

    def own_half(kk, carry):
        fin[blk(kk), :] = x_sum(yh, kk)

        @pl.when(kk == kk0)
        def _():
            h_copy(4).start()

        return carry

    lax.fori_loop(kk0, 5, own_half, 0)

    def z_of(kk):
        return (m_me + 8 - 4 + kk - off) % 8

    def f_copy(kk):
        return copy(fin.at[blk(kk), :], zin.at[z], f_s.at[kk], f_r.at[z], (z_of(kk) * 2 + yl, space))

    def f_start(kk):
        @pl.when(z_of(kk) != z)
        def _():
            f_copy(kk).start()

    def add_half(kk, carry):
        h_copy(kk).wait_recv()
        fin[blk(kk), :] = fin[blk(kk), :] + yin[blk(kk), :]

        @pl.when(kk > kk0)
        def _():
            f_start(kk - 1)

        return carry

    lax.fori_loop(kk0, 5, add_half, 0)
    f_start(4)

    k_me = (m_me + 8 - off - z) % 8
    d_me = 2 * (k_me + off) + core - yl
    mine = k_me < nb
    sends_mirror = mine & (d_me >= 1) & (d_me <= 7)
    mirror = copy(mout, minb, m_s, m_r, m_dev)

    @pl.when(mine)
    def _():
        total = fin[blk(4 - k_me), :]
        for dz in range(1, 8):
            zz = (z + dz) % 8
            copy(fin.at[blk(0), :], zin.at[zz], f_s.at[0], f_r.at[zz], (snap, space)).wait_recv()
            total = total + zin[zz]
        mout[...] = total
        o_ref[...] = total

    @pl.when(sends_mirror)
    def _():
        mirror.start()

    @pl.when(jnp.logical_not(mine))
    def _():
        mirror.wait_recv()
        o_ref[...] = minb[...].T

    @pl.when(space < 15)
    def _():
        for f in range(2):
            halo_down(f).wait_send()

    @pl.when(space > 0)
    def _():
        for f in range(2):
            halo_up(f).wait_send()

    for j in range(8):
        @pl.when(z != j)
        def _():
            z_copy(j).wait_send()

    def drain(zz, carry):
        y_copy(zz).wait_send()
        c_copy(0, zz).wait_send()
        c_copy(1, zz).wait_send()
        return carry

    lax.fori_loop(0, 8, drain, 0)

    def drain_blocks(kk, carry):
        for t in range(6):
            x_copy(m_of(t), kk).wait_send()
        h_copy(kk).wait_send()

        @pl.when(z_of(kk) != z)
        def _():
            f_copy(kk).wait_send()

        return carry

    lax.fori_loop(kk0, 5, drain_blocks, 0)

    @pl.when(sends_mirror)
    def _():
        mirror.wait_send()


def shards(factors, snapshots, lon_coeff, lat_coeff):
    x = jnp.transpose(snapshots, (1, 2, 3, 0)).reshape(8, NLON, B)
    coef = jnp.concatenate([lon_coeff.reshape(8, NLON), lat_coeff.reshape(8, NLON)], axis=0).T
    dma = pltpu.SemaphoreType.DMA
    vmem = pl.BlockSpec(memory_space=pltpu.VMEM)
    bf, f32 = jnp.bfloat16, jnp.float32
    return pl.pallas_call(
        kernel,
        out_shape=jax.ShapeDtypeStruct((B, B), f32),
        in_specs=[vmem, vmem, pl.BlockSpec(memory_space=pltpu.SMEM)],
        out_specs=vmem,
        scratch_shapes=[
            pltpu.VMEM((2, 2, NLON, B), bf),
            pltpu.VMEM((8, NLON + 16, B), f32),
            pltpu.VMEM((8, NLON, B), bf),
            pltpu.VMEM((2, 8, KPAD, B), bf),
            pltpu.VMEM((16 * B, KPAD), bf),
            pltpu.VMEM((8, 5 * B, B), f32),
            pltpu.VMEM((4, 2, 5 * B, B), f32),
            pltpu.VMEM((5 * B, B), f32),
            pltpu.VMEM((5 * B, B), f32),
            pltpu.VMEM((5 * B, B), f32),
            pltpu.VMEM((8, B, B), f32),
            pltpu.VMEM((B, B), f32),
            pltpu.VMEM((B, B), f32),
            dma((2, 2)), dma((2, 2)), dma,
            dma((8,)), dma((8,)),
            dma((8,)), dma((8,)),
            dma((2, 8)), dma((2, 8)),
            dma((8, 5)), dma((4, 2, 5)),
            dma((5,)), dma((5,)),
            dma((5,)), dma((8,)),
            dma, dma,
        ],
        compiler_params=pltpu.CompilerParams(collective_id=0, has_side_effects=True),
        name="gram",
    )(x, coef, jnp.asarray(factors))


def solution(mesh):
    factors = row_factors(2, 64, NLON)
    return jax.shard_map(
        functools.partial(shards, factors),
        mesh=mesh,
        in_specs=(P("snap", None, "space", None), P(None, "space", None), P(None, "space", None)),
        out_specs=P("snap", "space"),
        check_vma=False,
    )
```

time: 614 us -> 127 us (0.21)
  waiting for transfers between devices: 570 us -> 0 us
  Pallas kernels: 0 us -> 122 us
  between operations: 14.2 us -> 0.02 us
  matrix products: 12.5 us -> 0 us
  starting transfers between devices: 7.35 us -> 0 us
    all_gather x1 -> x0, waiting for transfers between devices: 490 us -> none  [shards(): lax.all_gather(scaled, 'snap', axis=0, tiled=True)]
    pallas_call x0 -> x1, Pallas kernels: none -> 122 us  [shards(): pl.pallas_call(kernel, out_shape=jax.ShapeDtypeStruct((B, B), f32), in_sp...]
    reduce_scatter x1 -> x0, waiting for transfers between devices: 74.6 us -> none  [shards(): lax.psum_scatter(partial_value, 'space', scatter_dimension=1, tiled=True)]
    dot_general x1 -> x0, matrix products: 12.5 us -> none  [inner_tile(): lax.dot_general(left, right, (((1,), (1,)), ((), ())), preferred_element_...]
    ppermute x2 -> x0, starting transfers between devices: 7.3 us -> none  [the longest x1 5.38 us: padded_2(): lax.ppermute(tail, axis, [(i, (i + 1) % count) for i in range(ends)])]
  transfers between devices with their start and end apart: 4 -> 0, of which waited for: 3 -> 0; matrix products, arithmetic and copies ran while one was open for 0% -> 0% of each run, Pallas kernels for 0% -> 0%
where the time goes in v1:
time: 127 us; the launch traced here: 126 us
  Pallas kernels  122 us (96%)
  local copies, waits for them, and re-layouts  3.87 us (3%)
    pallas_call x1, Pallas kernels, shards(): pl.pallas_call(kernel, out_shape=jax.ShapeDtypeStruct((B, B), f32), in_sp...  122 us

profile of v1, /device:TPU:33, one launch (start us, length us, event | category | flops | bytes accessed | tf_op | source)
XLA Modules:
  0.0 126.1 jit_solution(11987318602274158802)
XLA Ops:
  0.0 0.7 reshape.10
  0.8 0.8 reshape.11
  1.5 0.9 copy.9
  2.4 122.2 %gram.1 = f32[128,128]{1,0:T(8,128)} custom-call(bf16[8,720,128]{2,1,0:T(8,128)(2,1)} %bitcast.4, f32[720,16]{1,0:T(8,128)} %bitcast.5, f32[64]{0:T(128)} %constant.2.clone.fac_ref), custom_call_target="tpu_custom_call" | custom-call | tf_op jit(solution)/shard_map/gram/pallas_call | solution.py:383
  124.7 1.5 %copy.11 = f32[128,128]{1,0:T(8,128)} copy(f32[128,128]{1,0:T(8,128)} %gram.1) | data formatting | bytes 131072
  (1 shorter events, 0.0 us)

commit v2 on v1

--- a/solution.py
+++ b/solution.py
@@ -23,8 +23,8 @@
     return (np.sqrt(cosine) * total ** (-0.25)).astype(np.float32)
 
 
-def kernel(x_ref, coef_ref, fac_ref, o_ref,
-           halo, v32, sc, rows, a2, part, xin, q, yin, fin, zin, mout, minb,
+def kernel(x_ref, lon_ref, lat_ref, fac_ref, o_ref,
+           coef, halo, v32, sc, rows, a2, part, xin, q, yin, fin, zin, mout, minb,
            halo_s, halo_r, loc_s, z_s, z_r, y_s, y_r, c_s, c_r, x_s, x_r, h_s, h_r, f_s, f_r, m_s, m_r):
     snap = lax.axis_index("snap")
     space = lax.axis_index("space")
@@ -72,33 +72,11 @@
     def _():
         greet(m_dev)
 
-    pl.semaphore_wait(
-        barrier,
-        13 + (space > 0).astype(jnp.int32) + (space < 15).astype(jnp.int32) + (snap != space).astype(jnp.int32))
-
     def halo_down(f):
         return copy(x_ref.at[4 * f + 3], halo.at[0, f], halo_s.at[0, f], halo_r.at[0, f], dn_dev)
 
     def halo_up(f):
         return copy(x_ref.at[4 * f], halo.at[1, f], halo_s.at[1, f], halo_r.at[1, f], up_dev)
-
-    @pl.when(space < 15)
-    def _():
-        for f in range(2):
-            halo_down(f).start()
-
-    @pl.when(space > 0)
-    def _():
-        for f in range(2):
-            halo_up(f).start()
-
-    @pl.when(space == 0)
-    def _():
-        halo[0] = jnp.zeros((2, NLON, B), jnp.bfloat16)
-
-    @pl.when(space == 15)
-    def _():
-        halo[1] = jnp.zeros((2, NLON, B), jnp.bfloat16)
 
     def slot(yy, zz, cc):
         return rows.at[yy, zz, pl.ds(pl.multiple_of(cc * NLON, 16), NLON), :]
@@ -124,51 +102,85 @@
                 south = x_ref[j + 1, pl.ds(s, CH), :]
             lon_part = west + east - 2.0 * a
             lat_part = south.astype(jnp.float32) + north.astype(jnp.float32) - 2.0 * a
-            smooth = a + coef_ref[pl.ds(s, CH), j:j + 1] * lon_part + coef_ref[pl.ds(s, CH), 8 + j:9 + j] * lat_part
+            smooth = a + coef[pl.ds(s, CH), j:j + 1] * lon_part + coef[pl.ds(s, CH), 8 + j:9 + j] * lat_part
             sc[j, pl.ds(s, CH), :] = (smooth * scale).astype(jnp.bfloat16)
 
-    def z_copy(j):
-        return copy(sc.at[j], slot(yl, z, core), z_s.at[j], z_r.at[z], (j * 2 + yl, space))
-
-    def local_copy(j):
-        return pltpu.make_async_copy(sc.at[j], slot(yl, z, core), loc_s)
-
-    def z_start(j):
-        @pl.when(z == j)
-        def _():
-            local_copy(j).start()
-
-        @pl.when(z != j)
-        def _():
-            z_copy(j).start()
-
+    def j_of(zz):
+        return (zz + 8 - core) % 8
+
+    def z_copy(zz):
+        return copy(sc.at[j_of(zz)], slot(yl, z, core), z_s.at[zz], z_r.at[z], (zz * 2 + yl, space))
+
+    def local_copy():
+        return pltpu.make_async_copy(sc.at[j_of(z)], slot(yl, z, core), loc_s)
+
+    def near(i):
+        return (z + 8 + ((i + 1) // 2) * (2 * (i % 2) - 1)) % 8
+
+    coef[...] = jnp.concatenate([lon_ref[0], lon_ref[1], lat_ref[0], lat_ref[1]], axis=0).T
     rows[:, :, 2 * NLON:, :] = jnp.zeros((2, 8, KPAD - 2 * NLON, B), jnp.bfloat16)
 
-    last = None
+    @pl.when(space == 0)
+    def _():
+        halo[0] = jnp.zeros((2, NLON, B), jnp.bfloat16)
+
+    @pl.when(space == 15)
+    def _():
+        halo[1] = jnp.zeros((2, NLON, B), jnp.bfloat16)
+
     for j in (1, 2, 5, 6):
         stencil(j)
-        if last is not None:
-            z_start(last)
-        last = j
-
-    @pl.when(space > 0)
-    def _():
+
+    pl.semaphore_wait(
+        barrier,
+        13 + (space > 0).astype(jnp.int32) + (space < 15).astype(jnp.int32) + (snap != space).astype(jnp.int32))
+
+    @pl.when(core == 0)
+    def _():
+        for f in range(2):
+            halo_down(f).start()
+
+        @pl.when(space > 0)
+        def _():
+            for f in range(2):
+                halo_up(f).start()
+
+        for f in range(2):
+            halo_up(f).wait_recv()
+        stencil(3)
+        stencil(7)
+
+    @pl.when(core == 1)
+    def _():
+        for f in range(2):
+            halo_up(f).start()
+
+        @pl.when(space < 15)
+        def _():
+            for f in range(2):
+                halo_down(f).start()
+
         for f in range(2):
             halo_down(f).wait_recv()
-
-    @pl.when(space < 15)
-    def _():
-        for f in range(2):
-            halo_up(f).wait_recv()
-
-    for j in (0, 3, 4, 7):
-        stencil(j)
-        z_start(last)
-        last = j
-    z_start(last)
-
-    def near(i):
-        return (z + 8 + ((i + 1) // 2) * (2 * (i % 2) - 1)) % 8
+        stencil(0)
+        stencil(4)
+
+    def z_start(i, carry):
+        zz = near(i)
+
+        @pl.when(zz % 4 != 0)
+        def _():
+            @pl.when(i == 0)
+            def _():
+                local_copy().start()
+
+            @pl.when(i > 0)
+            def _():
+                z_copy(zz).start()
+
+        return carry
+
+    lax.fori_loop(0, 8, z_start, 0)
 
     def y_copy(zz):
         return copy(slot(yl, zz, core), slot(yl, zz, core), y_s.at[zz], y_r.at[zz], y_dev)
@@ -193,7 +205,7 @@
 
         @pl.when(i == 0)
         def _():
-            local_copy(0).wait()
+            local_copy().wait()
 
         @pl.when(i > 0)
         def _():
@@ -211,7 +223,46 @@
 
         return carry
 
-    lax.fori_loop(0, 8, step, 0)
+    early = jnp.where(z % 4 == 0, 0, 3)
+    lax.fori_loop(0, early, step, 0)
+
+    @pl.when(core == 0)
+    def _():
+        @pl.when(space > 0)
+        def _():
+            for f in range(2):
+                halo_down(f).wait_recv()
+
+        stencil(0)
+        stencil(4)
+
+    @pl.when(core == 1)
+    def _():
+        @pl.when(space < 15)
+        def _():
+            for f in range(2):
+                halo_up(f).wait_recv()
+
+        stencil(3)
+        stencil(7)
+
+    def z_start_late(i, carry):
+        zz = near(i)
+
+        @pl.when(zz % 4 == 0)
+        def _():
+            @pl.when(i == 0)
+            def _():
+                local_copy().start()
+
+            @pl.when(i > 0)
+            def _():
+                z_copy(zz).start()
+
+        return carry
+
+    lax.fori_loop(0, 8, z_start_late, 0)
+    lax.fori_loop(early, 8, step, 0)
     y_arrive(near(7))
     c_copy(1 - yl, near(7)).start()
     turn(near(7))
@@ -343,10 +394,8 @@
         for f in range(2):
             halo_up(f).wait_send()
 
-    for j in range(8):
-        @pl.when(z != j)
-        def _():
-            z_copy(j).wait_send()
+    for dz in range(1, 8):
+        z_copy((z + dz) % 8).wait_send()
 
     def drain(zz, carry):
         y_copy(zz).wait_send()
@@ -376,16 +425,16 @@
 
 def shards(factors, snapshots, lon_coeff, lat_coeff):
     x = jnp.transpose(snapshots, (1, 2, 3, 0)).reshape(8, NLON, B)
-    coef = jnp.concatenate([lon_coeff.reshape(8, NLON), lat_coeff.reshape(8, NLON)], axis=0).T
     dma = pltpu.SemaphoreType.DMA
     vmem = pl.BlockSpec(memory_space=pltpu.VMEM)
     bf, f32 = jnp.bfloat16, jnp.float32
     return pl.pallas_call(
         kernel,
         out_shape=jax.ShapeDtypeStruct((B, B), f32),
-        in_specs=[vmem, vmem, pl.BlockSpec(memory_space=pltpu.SMEM)],
+        in_specs=[vmem, vmem, vmem, pl.BlockSpec(memory_space=pltpu.SMEM)],
         out_specs=vmem,
         scratch_shapes=[
+            pltpu.VMEM((NLON, 16), f32),
             pltpu.VMEM((2, 2, NLON, B), bf),
             pltpu.VMEM((8, NLON + 16, B), f32),
             pltpu.VMEM((8, NLON, B), bf),
@@ -410,7 +459,7 @@
         ],
         compiler_params=pltpu.CompilerParams(collective_id=0, has_side_effects=True),
         name="gram",
-    )(x, coef, jnp.asarray(factors))
+    )(x, lon_coeff, lat_coeff, jnp.asarray(factors))
 
 
 def solution(mesh):

time: 127 us -> 132 us (1.039)
  Pallas kernels: 122 us -> 130 us
  local copies, waits for them, and re-layouts: 3.87 us -> 1.47 us
    pallas_call x1, Pallas kernels: 122 us -> 130 us  [shards(): pl.pallas_call(kernel, out_shape=jax.ShapeDtypeStruct((B, B), f32), in_sp...]
    reshape x2 -> x0, local copies, waits for them, and re-layouts: 1.5 us -> none  [the longest x1 0.75 us: shards(): lat_coeff.reshape(8, NLON)]
where the time goes in v2:
time: 132 us; the launch traced here: 131 us
  Pallas kernels  130 us (98%)
  local copies, waits for them, and re-layouts  1.47 us (1%)
    pallas_call x1, Pallas kernels, shards(): pl.pallas_call(kernel, out_shape=jax.ShapeDtypeStruct((B, B), f32), in_sp...  130 us

profile of v2, /device:TPU:33, one launch (start us, length us, event | category | flops | bytes accessed | tf_op | source)
XLA Modules:
  0.0 131.4 jit_solution(17570862989741424858)
XLA Ops:
  0.0 130.0 %gram.1 = f32[128,128]{1,0:T(8,128)} custom-call(bf16[8,720,128]{2,1,0:T(8,128)(2,1)} %bitcast.3, f32[2,4,720]{2,1,0:T(4,128)} %lon_ref.1, f32[2,4,720]{2,1,0:T(4,128)} %lat_ref.1, f32[64]{0:T(128)} %constant.2.clone.fac_ref), custom_call_target="tpu_custom_call" | custom-call | tf_op jit(solution)/shard_map/gram/pallas_call | solution.py:431
  130.0 1.5 %copy.6 = f32[128,128]{1,0:T(8,128)} copy(f32[128,128]{1,0:T(8,128)} %gram.1) | data formatting | bytes 131072

commit v3 on v0

v3 whole, which is shorter than its diff:
```python
import functools
import math

import jax
import jax.numpy as jnp
import numpy as np
from jax import lax
from jax.experimental import pallas as pl
from jax.experimental.pallas import tpu as pltpu
from jax.sharding import PartitionSpec as P

MESH = pl.DeviceIdType.MESH
NLON = 720
KPAD = 1536
B = 128
CH = 144
QT = B // 4
EARLY, LATE = 528, 192
ORDER = [(word[:1], int(word[1:])) for word in (
    "l0", "z1", "z2", "t0", "y0", "w1", "w2", "z3", "z4", "t1", "y1", "t2", "s0", "y2", "w3", "w4", "z5", "z6",
    "h0", "L0", "Z1", "Z2", "Z3", "Z4", "Z5", "Z6", "Z7", "T0", "Y0", "t3", "s1", "y3", "t4", "s2", "y4", "S0",
    "T1", "Y1", "T2", "Y2", "p0", "s3", "S1", "p1", "S2", "p2", "T3", "Y3", "T4", "Y4", "w5", "w6", "z7", "t5",
    "y5", "t6", "y6", "s4", "S3", "p3", "x0", "S4", "p4", "x1", "T5", "Y5", "T6", "Y6", "T7", "t7", "y7", "Y7",
    "s5", "S5", "p5", "x2", "x3", "s6", "S6", "p6", "x4", "x5", "s7", "S7", "p7", "x6", "x7",
)]


def row_factors(fields, nlat, nlon):
    lat = (45.0 + 0.5 * (np.arange(nlat) + 0.5 - nlat / 2.0)) * (math.pi / 180.0)
    cosine = np.cos(lat)
    total = fields * nlon * cosine.sum()
    return (np.sqrt(cosine) * total ** (-0.25)).astype(np.float32)


def kernel(x_ref, lon_ref, lat_ref, fac_ref, o_ref,
           coef, halo, v32, sc, rows, a2, part, xin, fin, zin, tot, obuf, minb,
           halo_s, halo_r, loc_s, z_s, z_r, y_s, y_r, c_s, c_r, x_s, x_r, f_s, f_r,
           o_s, o_r, m_s, m_r):
    snap = lax.axis_index("snap")
    space = lax.axis_index("space")
    z, yl = snap // 2, snap % 2
    xx, yh, core = space // 4, (space // 2) % 2, space % 2
    m_me = space // 2
    same = (core == yl).astype(jnp.int32)
    nb = 4 + same
    kk0 = 1 - same
    off = jnp.where(same == 1, 0, yl)

    def copy(src, dst, ss, rs, dev):
        return pltpu.make_async_remote_copy(
            src_ref=src, dst_ref=dst, send_sem=ss, recv_sem=rs, device_id=dev, device_id_type=MESH)

    up_dev = (snap, jnp.maximum(space - 1, 0))
    dn_dev = (snap, jnp.minimum(space + 1, 15))
    y_dev = (z * 2 + 1 - yl, space)
    c_dev = (snap, m_me * 2 + 1 - core)
    h_dev = (snap, xx * 4 + (1 - yh) * 2 + core)

    barrier = pltpu.get_barrier_semaphore()

    def greet(dev):
        pl.semaphore_signal(barrier, inc=1, device_id=dev, device_id_type=MESH)

    for dz in range(1, 8):
        greet((((z + dz) % 8) * 2 + yl, space))
        greet((((z + dz) % 8) * 2 + yl, h_dev[1]))
    for dx in range(1, 4):
        greet((snap, ((xx + dx) % 4) * 4 + yh * 2 + core))
    greet(y_dev)
    greet(c_dev)
    greet(h_dev)

    @pl.when(space > 0)
    def _():
        greet(up_dev)

    @pl.when(space < 15)
    def _():
        greet(dn_dev)

    def halo_down(f):
        return copy(x_ref.at[4 * f + 3], halo.at[0, f], halo_s.at[0, f], halo_r.at[0, f], dn_dev)

    def halo_up(f):
        return copy(x_ref.at[4 * f], halo.at[1, f], halo_s.at[1, f], halo_r.at[1, f], up_dev)

    def span(late):
        return LATE if late else EARLY

    def slot(yy, zz, cc, late):
        return rows.at[yy, zz, pl.ds(pl.multiple_of(cc * NLON + late * EARLY, 16), span(late)), :]

    def stencil(j, place):
        f, row = divmod(j, 4)
        v = x_ref[j].astype(jnp.float32)
        v32[j, pl.ds(8, NLON), :] = v
        v32[j, 7:8, :] = v[NLON - 1:, :]
        v32[j, NLON + 8:NLON + 9, :] = v[:1, :]
        scale = fac_ref[space * 4 + row]
        for s in range(0, NLON, CH):
            a = v32[j, pl.ds(8 + s, CH), :]
            west = v32[j, pl.ds(7 + s, CH), :]
            east = v32[j, pl.ds(9 + s, CH), :]
            if row == 0:
                north = halo[0, f, pl.ds(s, CH), :]
            else:
                north = x_ref[j - 1, pl.ds(s, CH), :]
            if row == 3:
                south = halo[1, f, pl.ds(s, CH), :]
            else:
                south = x_ref[j + 1, pl.ds(s, CH), :]
            lon_part = west + east - 2.0 * a
            lat_part = south.astype(jnp.float32) + north.astype(jnp.float32) - 2.0 * a
            smooth = a + coef[pl.ds(s, CH), j:j + 1] * lon_part + coef[pl.ds(s, CH), 8 + j:9 + j] * lat_part
            sc[pl.ds(place * NLON + s, CH), :] = (smooth * scale).astype(jnp.bfloat16)

    def mine_for(zz, late):
        return sc.at[pl.ds(pl.multiple_of(late * 8 * EARLY + zz * span(late), 16), span(late)), :]

    def z_copy(zz, late):
        return copy(mine_for(zz, late), slot(yl, z, core, late), z_s.at[late, zz], z_r.at[late, z],
                    (zz * 2 + yl, space))

    def local_copy(late):
        return pltpu.make_async_copy(mine_for(z, late), slot(yl, z, core, late), loc_s.at[late])

    def near(i):
        return (z + 8 + ((i + 1) // 2) * (2 * (i % 2) - 1)) % 8

    coef[...] = jnp.concatenate([lon_ref[0], lon_ref[1], lat_ref[0], lat_ref[1]], axis=0).T
    rows[:, :, 2 * NLON:, :] = jnp.zeros((2, 8, KPAD - 2 * NLON, B), jnp.bfloat16)

    @pl.when(space == 0)
    def _():
        halo[0] = jnp.zeros((2, NLON, B), jnp.bfloat16)

    @pl.when(space == 15)
    def _():
        halo[1] = jnp.zeros((2, NLON, B), jnp.bfloat16)

    for place, j in enumerate((1, 2, 5, 6)):
        stencil(j, place)

    pl.semaphore_wait(
        barrier,
        20 + (space > 0).astype(jnp.int32) + (space < 15).astype(jnp.int32))

    @pl.when(space < 15)
    def _():
        for f in range(2):
            halo_down(f).start()

    @pl.when(space > 0)
    def _():
        for f in range(2):
            halo_up(f).start()

    @pl.when(core == 0)
    def _():
        for f in range(2):
            halo_up(f).wait_recv()
            stencil(4 * f + 3, 4 + f)

    @pl.when(core == 1)
    def _():
        for f in range(2):
            halo_down(f).wait_recv()
            stencil(4 * f, 4 + f)

    def rest_of_band(n):
        @pl.when(core == 0)
        def _():
            @pl.when(space > 0)
            def _():
                for f in range(2):
                    halo_down(f).wait_recv()

            for f in range(2):
                stencil(4 * f, 6 + f)

        @pl.when(core == 1)
        def _():
            @pl.when(space < 15)
            def _():
                for f in range(2):
                    halo_up(f).wait_recv()

            for f in range(2):
                stencil(4 * f + 3, 6 + f)

    def y_copy(yy, zz, late):
        block = slot(yy, zz, core, late)
        return copy(block, block, y_s.at[late, zz], y_r.at[late, zz], y_dev)

    def c_copy(yy, zz, cc, late):
        block = slot(yy, zz, cc, late)
        return copy(block, block, c_s.at[late, yy, zz], c_r.at[late, yy, zz], c_dev)

    def c_arrive(yy, zz):
        for late in range(2):
            c_copy(yy, zz, 1 - core, late).wait_recv()

    def turn(zz):
        c_arrive(yl, zz)
        a2[blk(zz), :] = rows[yl, zz].T

    def blk(kk):
        return pl.ds(pl.multiple_of(kk * B, B), B)

    def quarter(kk, to):
        return pl.ds(pl.multiple_of(kk * B + to * QT, QT), QT)

    def x_copy(m, kk, dx):
        to = (xx + dx) % 4
        return copy(part.at[m, quarter(kk, to), :], xin.at[m, kk, 3 - dx], x_s.at[m, kk], x_r.at[m, kk],
                    (snap, to * 4 + yh * 2 + core))

    def x_all(m, kk):
        whole = xin.at[m, kk]
        return copy(whole, whole, x_s.at[m, kk], x_r.at[m, kk], (snap, space))

    def z_of(m, kk):
        return (m + 8 - 4 + kk - off) % 8

    def f_start(m, kk, r):
        to, yy = z_of(m, kk), m % 2
        here, there = fin.at[m, kk], zin.at[m // 2, z, yh]

        @pl.when((to == z) & (yy == yh))
        def _():
            pltpu.make_async_copy(here, there, f_r.at[m // 2]).start()

        @pl.when((to != z) | (yy != yh))
        def _():
            copy(here, there, f_s.at[m, kk], f_r.at[m // 2], (to * 2 + yl, xx * 4 + yy * 2 + core)).start()

    def take(n, late):
        zz = near(n)
        if n == 0:
            local_copy(late).wait()
        else:
            block = slot(yl, zz, core, late)
            copy(block, block, z_s.at[late, zz], z_r.at[late, zz], (snap, space)).wait_recv()
        c_copy(yl, zz, core, late).start()

    def share(n, late):
        y_copy(1 - yl, near(n), late).wait_recv()
        c_copy(1 - yl, near(n), core, late).start()

    def pairs(t, use):
        u = near(t)

        def one(n, carry):
            w = near(n)
            k1 = (u + 8 - w - off) % 8
            k2 = (w + 8 - u - off) % 8

            @pl.when(k1 < nb)
            def _():
                use(u, 4 - k1, w)

            @pl.when((n < t) & (k2 < nb))
            def _():
                use(w, 4 - k2, u)

            return carry

        lax.fori_loop(0, t + 1, one, 0)

    def multiply(m, kk, r):
        part[m, blk(kk), :] = jnp.dot(a2[blk(r), :], rows[core, m], preferred_element_type=jnp.float32)

    def send(m, kk, r):
        for dx in range(1, 4):
            x_copy(m, kk, dx).start()

    def add(m, kk, r):
        x_all(m, kk).wait_recv()
        fin[m, kk] = part[m, quarter(kk, xx), :] + xin[m, kk, 0] + xin[m, kk, 1] + xin[m, kk, 2]

    def products(t):
        turn(near(t))
        c_arrive(1 - yl, near(t))
        pairs(t, multiply)
        pairs(t, send)

    def x_sum(t):
        pairs(t, add)
        pairs(t, f_start)

    actions = {"h": rest_of_band, "p": products, "x": x_sum}
    for late, names in enumerate(("lztysw", "LZTYSW")):
        for name, action in zip(names, (
                lambda n, late: local_copy(late).start(),
                lambda n, late: z_copy(near(n), late).start(),
                take,
                lambda n, late: y_copy(yl, near(n), late).start(),
                share,
                lambda n, late: z_copy(near(n), late).wait_send())):
            actions[name] = functools.partial(action, late=late)
    for name, n in ORDER:
        actions[name](n)

    def column(n):
        mx = (xx + n) % 4
        m = 2 * mx + yh
        k = (m + 8 - off - z) % 8
        d = 2 * (k + off) + core - yl
        return mx, m, k < nb, (k < nb) & (d >= 1) & (d <= 7)

    rowq = pl.ds(pl.multiple_of(xx * QT, QT), QT)

    def o_copy(n):
        mx, m, _, _ = column(n)
        return copy(tot.at[mx], obuf.at[rowq, :], o_s.at[mx], o_r, (snap, mx * 4 + yh * 2 + core))

    def m_copy(n):
        mx, m, _, _ = column(n)
        return copy(tot.at[mx], minb.at[rowq, :], m_s.at[mx], m_r, (m * 2 + core, snap))

    for n in (1, 2, 3, 0):
        mx, m, mine, mirrored = column(n)

        @pl.when(mine)
        def _():
            pltpu.make_async_copy(zin.at[mx], zin.at[mx], f_r.at[mx]).wait()
            total = zin[mx, 0, 0]
            for zz in range(8):
                for yy in range(2):
                    if zz + yy:
                        total = total + zin[mx, zz, yy]
            tot[mx] = total

    for n in (1, 2, 3, 0):
        mx, m, mine, mirrored = column(n)

        @pl.when(mirrored)
        def _():
            m_copy(n).start()

        @pl.when(mine)
        def _():
            if n:
                o_copy(n).start()
            else:
                pltpu.make_async_copy(tot.at[mx], obuf.at[rowq, :], o_r).start()

    k_me = (m_me + 8 - off - z) % 8

    @pl.when(k_me < nb)
    def _():
        pltpu.make_async_copy(obuf, obuf, o_r).wait()
        o_ref[...] = obuf[...]

    @pl.when(k_me >= nb)
    def _():
        pltpu.make_async_copy(minb, minb, m_r).wait()
        o_ref[...] = minb[...].T

    @pl.when(space < 15)
    def _():
        for f in range(2):
            halo_down(f).wait_send()

    @pl.when(space > 0)
    def _():
        for f in range(2):
            halo_up(f).wait_send()

    for n in range(1, 8):
        for late in range(2):
            if ("wW"[late], n) not in ORDER:
                z_copy(near(n), late).wait_send()

    def drain(zz, carry):
        for late in range(2):
            y_copy(yl, zz, late).wait_send()
            c_copy(0, zz, core, late).wait_send()
            c_copy(1, zz, core, late).wait_send()
        return carry

    lax.fori_loop(0, 8, drain, 0)

    def drain_blocks(kk, carry):
        def one(m, c):
            x_all(m, kk).wait_send()

            @pl.when((z_of(m, kk) != z) | (m % 2 != yh))
            def _():
                copy(fin.at[m, kk], fin.at[m, kk], f_s.at[m, kk], f_r.at[0], (snap, space)).wait_send()

            return c

        return lax.fori_loop(0, 8, one, carry)

    lax.fori_loop(kk0, 5, drain_blocks, 0)

    for n in range(4):
        mx, m, mine, mirrored = column(n)

        @pl.when(mirrored)
        def _():
            m_copy(n).wait_send()

        if n:
            @pl.when(mine)
            def _():
                o_copy(n).wait_send()


def shards(factors, snapshots, lon_coeff, lat_coeff):
    x = jnp.transpose(snapshots, (1, 2, 3, 0)).reshape(8, NLON, B)
    dma = pltpu.SemaphoreType.DMA
    vmem = pl.BlockSpec(memory_space=pltpu.VMEM)
    bf, f32 = jnp.bfloat16, jnp.float32
    return pl.pallas_call(
        kernel,
        out_shape=jax.ShapeDtypeStruct((B, B), f32),
        in_specs=[vmem, vmem, vmem, pl.BlockSpec(memory_space=pltpu.SMEM)],
        out_specs=vmem,
        scratch_shapes=[
            pltpu.VMEM((NLON, 16), f32),
            pltpu.VMEM((2, 2, NLON, B), bf),
            pltpu.VMEM((8, NLON + 16, B), f32),
            pltpu.VMEM((8 * NLON, B), bf),
            pltpu.VMEM((2, 8, KPAD, B), bf),
            pltpu.VMEM((8 * B, KPAD), bf),
            pltpu.VMEM((8, 5 * B, B), f32),
            pltpu.VMEM((8, 5, 3, QT, B), f32),
            pltpu.VMEM((8, 5, QT, B), f32),
            pltpu.VMEM((4, 8, 2, QT, B), f32),
            pltpu.VMEM((4, QT, B), f32),
            pltpu.VMEM((B, B), f32),
            pltpu.VMEM((B, B), f32),
            dma((2, 2)), dma((2, 2)), dma((2,)),
            dma((2, 8)), dma((2, 8)),
            dma((2, 8)), dma((2, 8)),
            dma((2, 2, 8)), dma((2, 2, 8)),
            dma((8, 5)), dma((8, 5)),
            dma((8, 5)), dma((4,)),
            dma((4,)), dma, dma((4,)), dma,
        ],
        compiler_params=pltpu.CompilerParams(collective_id=0, has_side_effects=True),
        name="gram",
    )(x, lon_coeff, lat_coeff, jnp.asarray(factors))


def solution(mesh):
    factors = row_factors(2, 64, NLON)
    return jax.shard_map(
        functools.partial(shards, factors),
        mesh=mesh,
        in_specs=(P("snap", None, "space", None), P(None, "space", None), P(None, "space", None)),
        out_specs=P("snap", "space"),
        check_vma=False,
    )
```

time: 614 us -> 100 us (0.16)
  the two profiles are of different devices: /device:TPU:33 before, /device:TPU:5 now
where the time goes in v3:
time: 100 us
  Pallas kernels  98.6 us (99%)
  local copies, waits for them, and re-layouts  1.47 us (1%)
    pallas_call x1, Pallas kernels, shards(): pl.pallas_call(kernel, out_shape=jax.ShapeDtypeStruct((B, B), f32), in_sp...  98.6 us

profile of v3, /device:TPU:5, one launch (start us, length us, event | category | flops | bytes accessed | tf_op | source)
XLA Modules:
  0.0 100.1 jit_solution(12740505150146585367)
XLA Ops:
  0.0 98.6 %gram.1 = f32[128,128]{1,0:T(8,128)} custom-call(bf16[8,720,128]{2,1,0:T(8,128)(2,1)} %bitcast.3, f32[2,4,720]{2,1,0:T(4,128)} %lon_ref.1, f32[2,4,720]{2,1,0:T(4,128)} %lat_ref.1, f32[64]{0:T(128)} %constant.2.clone.fac_ref), custom_call_target="tpu_custom_call" | custom-call | tf_op jit(solution)/shard_map/gram/pallas_call | solution.py:416
  98.6 1.5 %copy.6 = f32[128,128]{1,0:T(8,128)} copy(f32[128,128]{1,0:T(8,128)} %gram.1) | data formatting | bytes 131072

commit v4 on v3

--- a/solution.py
+++ b/solution.py
@@ -18,10 +18,10 @@
 EARLY, LATE = 528, 192
 ORDER = [(word[:1], int(word[1:])) for word in (
     "l0", "z1", "z2", "t0", "y0", "w1", "w2", "z3", "z4", "t1", "y1", "t2", "s0", "y2", "w3", "w4", "z5", "z6",
-    "h0", "L0", "Z1", "Z2", "Z3", "Z4", "Z5", "Z6", "Z7", "T0", "Y0", "t3", "s1", "y3", "t4", "s2", "y4", "S0",
-    "T1", "Y1", "T2", "Y2", "p0", "s3", "S1", "p1", "S2", "p2", "T3", "Y3", "T4", "Y4", "w5", "w6", "z7", "t5",
-    "y5", "t6", "y6", "s4", "S3", "p3", "x0", "S4", "p4", "x1", "T5", "Y5", "T6", "Y6", "T7", "t7", "y7", "Y7",
-    "s5", "S5", "p5", "x2", "x3", "s6", "S6", "p6", "x4", "x5", "s7", "S7", "p7", "x6", "x7",
+    "h0", "L0", "Z1", "Z2", "Z3", "Z4", "Z5", "Z6", "T0", "Y0", "t3", "s1", "y3", "t4", "s2", "y4", "z7", "Z7",
+    "S0", "T1", "Y1", "T2", "Y2", "p0", "s3", "S1", "p1", "S2", "p2", "T3", "Y3", "T4", "Y4", "x0", "t5", "y5",
+    "t6", "y6", "s4", "S3", "p3", "x1", "S4", "p4", "x2", "T5", "Y5", "T6", "Y6", "T7", "t7", "y7", "Y7", "s5",
+    "S5", "p5", "x3", "s6", "S6", "p6", "x4", "s7", "S7", "p7", "x5", "x6", "x7",
 )]
 
 
@@ -32,9 +32,9 @@
     return (np.sqrt(cosine) * total ** (-0.25)).astype(np.float32)
 
 
-def kernel(x_ref, lon_ref, lat_ref, fac_ref, o_ref,
-           coef, halo, v32, sc, rows, a2, part, xin, fin, zin, tot, obuf, minb,
-           halo_s, halo_r, loc_s, z_s, z_r, y_s, y_r, c_s, c_r, x_s, x_r, f_s, f_r,
+def kernel(x_hbm, lon_ref, lat_ref, fac_ref, o_ref,
+           x_ref, coef, halo, v32, sc, rows, a2, part, xin, fin, zin, tot, obuf, minb,
+           load_s, halo_s, halo_r, loc_s, z_s, z_r, y_s, y_r, c_s, c_r, x_s, x_r, f_s, f_r,
            o_s, o_r, m_s, m_r):
     snap = lax.axis_index("snap")
     space = lax.axis_index("space")
@@ -46,6 +46,12 @@
     kk0 = 1 - same
     off = jnp.where(same == 1, 0, yl)
 
+    def load(j):
+        return pltpu.make_async_copy(x_hbm.at[j], x_ref.at[j], load_s.at[j])
+
+    for j in (1, 2, 0, 3, 5, 6, 4, 7):
+        load(j).start()
+
     def copy(src, dst, ss, rs, dev):
         return pltpu.make_async_remote_copy(
             src_ref=src, dst_ref=dst, send_sem=ss, recv_sem=rs, device_id=dev, device_id_type=MESH)
@@ -61,9 +67,8 @@
     def greet(dev):
         pl.semaphore_signal(barrier, inc=1, device_id=dev, device_id_type=MESH)
 
-    for dz in range(1, 8):
+    for dz in (1, 2, 6, 7):
         greet((((z + dz) % 8) * 2 + yl, space))
-        greet((((z + dz) % 8) * 2 + yl, h_dev[1]))
     for dx in range(1, 4):
         greet((snap, ((xx + dx) % 4) * 4 + yh * 2 + core))
     greet(y_dev)
@@ -79,10 +84,10 @@
         greet(dn_dev)
 
     def halo_down(f):
-        return copy(x_ref.at[4 * f + 3], halo.at[0, f], halo_s.at[0, f], halo_r.at[0, f], dn_dev)
+        return copy(x_hbm.at[4 * f + 3], halo.at[0, f], halo_s.at[0, f], halo_r.at[0, f], dn_dev)
 
     def halo_up(f):
-        return copy(x_ref.at[4 * f], halo.at[1, f], halo_s.at[1, f], halo_r.at[1, f], up_dev)
+        return copy(x_hbm.at[4 * f], halo.at[1, f], halo_s.at[1, f], halo_r.at[1, f], up_dev)
 
     def span(late):
         return LATE if late else EARLY
@@ -138,12 +143,18 @@
     def _():
         halo[1] = jnp.zeros((2, NLON, B), jnp.bfloat16)
 
-    for place, j in enumerate((1, 2, 5, 6)):
-        stencil(j, place)
+    for j in (1, 2, 0, 3):
+        load(j).wait()
+    stencil(1, 0)
+    stencil(2, 1)
+    for j in (5, 6, 4, 7):
+        load(j).wait()
+    stencil(5, 2)
+    stencil(6, 3)
 
     pl.semaphore_wait(
         barrier,
-        20 + (space > 0).astype(jnp.int32) + (space < 15).astype(jnp.int32))
+        10 + (space > 0).astype(jnp.int32) + (space < 15).astype(jnp.int32))
 
     @pl.when(space < 15)
     def _():
@@ -247,25 +258,33 @@
         y_copy(1 - yl, near(n), late).wait_recv()
         c_copy(1 - yl, near(n), core, late).start()
 
-    def pairs(t, use):
+    def pairs(t, use, then):
         u = near(t)
 
-        def one(n, carry):
+        def each(n, what):
             w = near(n)
             k1 = (u + 8 - w - off) % 8
             k2 = (w + 8 - u - off) % 8
 
             @pl.when(k1 < nb)
             def _():
-                use(u, 4 - k1, w)
+                what(u, 4 - k1, w)
 
             @pl.when((n < t) & (k2 < nb))
             def _():
-                use(w, 4 - k2, u)
+                what(w, 4 - k2, u)
+
+        def one(n, carry):
+            each(n, use)
+
+            @pl.when(n > 0)
+            def _():
+                each(n - 1, then)
 
             return carry
 
         lax.fori_loop(0, t + 1, one, 0)
+        each(t, then)
 
     def multiply(m, kk, r):
         part[m, blk(kk), :] = jnp.dot(a2[blk(r), :], rows[core, m], preferred_element_type=jnp.float32)
@@ -281,12 +300,10 @@
     def products(t):
         turn(near(t))
         c_arrive(1 - yl, near(t))
-        pairs(t, multiply)
-        pairs(t, send)
+        pairs(t, multiply, send)
 
     def x_sum(t):
-        pairs(t, add)
-        pairs(t, f_start)
+        pairs(t, add, f_start)
 
     actions = {"h": rest_of_band, "p": products, "x": x_sum}
     for late, names in enumerate(("lztysw", "LZTYSW")):
@@ -301,6 +318,39 @@
     for name, n in ORDER:
         actions[name](n)
 
+    @pl.when(space < 15)
+    def _():
+        for f in range(2):
+            halo_down(f).wait_send()
+
+    @pl.when(space > 0)
+    def _():
+        for f in range(2):
+            halo_up(f).wait_send()
+
+    for n in range(1, 8):
+        for late in range(2):
+            if ("wW"[late], n) not in ORDER:
+                z_copy(near(n), late).wait_send()
+
+    def drain(zz, carry):
+        for late in range(2):
+            y_copy(yl, zz, late).wait_send()
+            c_copy(0, zz, core, late).wait_send()
+            c_copy(1, zz, core, late).wait_send()
+        return carry
+
+    lax.fori_loop(0, 8, drain, 0)
+
+    def x_over(kk, carry):
+        def one(m, c):
+            x_all(m, kk).wait_send()
+            return c
+
+        return lax.fori_loop(0, 8, one, carry)
+
+    lax.fori_loop(kk0, 5, x_over, 0)
+
     def column(n):
         mx = (xx + n) % 4
         m = 2 * mx + yh
@@ -318,7 +368,7 @@
         mx, m, _, _ = column(n)
         return copy(tot.at[mx], minb.at[rowq, :], m_s.at[mx], m_r, (m * 2 + core, snap))
 
-    for n in (1, 2, 3, 0):
+    def whole(n):
         mx, m, mine, mirrored = column(n)
 
         @pl.when(mine)
@@ -331,7 +381,7 @@
                         total = total + zin[mx, zz, yy]
             tot[mx] = total
 
-    for n in (1, 2, 3, 0):
+    def place(n):
         mx, m, mine, mirrored = column(n)
 
         @pl.when(mirrored)
@@ -345,6 +395,39 @@
             else:
                 pltpu.make_async_copy(tot.at[mx], obuf.at[rowq, :], o_r).start()
 
+    whole(2)
+    whole(1)
+    place(2)
+    whole(3)
+    place(1)
+    whole(0)
+    place(3)
+    place(0)
+
+    def f_over(kk, carry):
+        def one(m, c):
+            @pl.when((z_of(m, kk) != z) | (m % 2 != yh))
+            def _():
+                copy(fin.at[m, kk], fin.at[m, kk], f_s.at[m, kk], f_r.at[0], (snap, space)).wait_send()
+
+            return c
+
+        return lax.fori_loop(0, 8, one, carry)
+
+    lax.fori_loop(kk0, 5, f_over, 0)
+
+    for n in range(4):
+        mx, m, mine, mirrored = column(n)
+
+        @pl.when(mirrored)
+        def _():
+            m_copy(n).wait_send()
+
+        if n:
+            @pl.when(mine)
+            def _():
+                o_copy(n).wait_send()
+
     k_me = (m_me + 8 - off - z) % 8
 
     @pl.when(k_me < nb)
@@ -356,56 +439,6 @@
     def _():
         pltpu.make_async_copy(minb, minb, m_r).wait()
         o_ref[...] = minb[...].T
-
-    @pl.when(space < 15)
-    def _():
-        for f in range(2):
-            halo_down(f).wait_send()
-
-    @pl.when(space > 0)
-    def _():
-        for f in range(2):
-            halo_up(f).wait_send()
-
-    for n in range(1, 8):
-        for late in range(2):
-            if ("wW"[late], n) not in ORDER:
-                z_copy(near(n), late).wait_send()
-
-    def drain(zz, carry):
-        for late in range(2):
-            y_copy(yl, zz, late).wait_send()
-            c_copy(0, zz, core, late).wait_send()
-            c_copy(1, zz, core, late).wait_send()
-        return carry
-
-    lax.fori_loop(0, 8, drain, 0)
-
-    def drain_blocks(kk, carry):
-        def one(m, c):
-            x_all(m, kk).wait_send()
-
-            @pl.when((z_of(m, kk) != z) | (m % 2 != yh))
-            def _():
-                copy(fin.at[m, kk], fin.at[m, kk], f_s.at[m, kk], f_r.at[0], (snap, space)).wait_send()
-
-            return c
-
-        return lax.fori_loop(0, 8, one, carry)
-
-    lax.fori_loop(kk0, 5, drain_blocks, 0)
-
-    for n in range(4):
-        mx, m, mine, mirrored = column(n)
-
-        @pl.when(mirrored)
-        def _():
-            m_copy(n).wait_send()
-
-        if n:
-            @pl.when(mine)
-            def _():
-                o_copy(n).wait_send()
 
 
 def shards(factors, snapshots, lon_coeff, lat_coeff):
@@ -416,9 +449,10 @@
     return pl.pallas_call(
         kernel,
         out_shape=jax.ShapeDtypeStruct((B, B), f32),
-        in_specs=[vmem, vmem, vmem, pl.BlockSpec(memory_space=pltpu.SMEM)],
+        in_specs=[pl.BlockSpec(memory_space=pl.ANY), vmem, vmem, pl.BlockSpec(memory_space=pltpu.SMEM)],
         out_specs=vmem,
         scratch_shapes=[
+            pltpu.VMEM((8, NLON, B), bf),
             pltpu.VMEM((NLON, 16), f32),
             pltpu.VMEM((2, 2, NLON, B), bf),
             pltpu.VMEM((8, NLON + 16, B), f32),
@@ -432,7 +466,7 @@
             pltpu.VMEM((4, QT, B), f32),
             pltpu.VMEM((B, B), f32),
             pltpu.VMEM((B, B), f32),
-            dma((2, 2)), dma((2, 2)), dma((2,)),
+            dma((8,)), dma((2, 2)), dma((2, 2)), dma((2,)),
             dma((2, 8)), dma((2, 8)),
             dma((2, 8)), dma((2, 8)),
             dma((2, 2, 8)), dma((2, 2, 8)),

time: 100 us -> 94.1 us (0.941)
  the two profiles are of different devices: /device:TPU:5 before, /device:TPU:33 now
where the time goes in v4:
time: 94.1 us; the launch traced here: 93.3 us
  Pallas kernels  91.8 us (98%)
  local copies, waits for them, and re-layouts  1.47 us (2%)
    pallas_call x1, Pallas kernels, shards(): pl.pallas_call(kernel, out_shape=jax.ShapeDtypeStruct((B, B), f32), in_sp...  91.8 us

profile of v4, /device:TPU:33, one launch (start us, length us, event | category | flops | bytes accessed | tf_op | source)
XLA Modules:
  0.0 93.3 jit_solution(10192145930403979018)
XLA Ops:
  0.0 91.8 %gram.1 = f32[128,128]{1,0:T(8,128)} custom-call(bf16[8,720,128]{2,1,0:T(8,128)(2,1)} %bitcast.3, f32[2,4,720]{2,1,0:T(4,128)} %lon_ref.1, f32[2,4,720]{2,1,0:T(4,128)} %lat_ref.1, f32[64]{0:T(128)} %constant.2.clone.fac_ref), custom_call_target="tpu_custom_call" | custom-call | tf_op jit(solution)/shard_map/gram/pallas_call | solution.py:449
  91.8 1.5 %copy.6 = f32[128,128]{1,0:T(8,128)} copy(f32[128,128]{1,0:T(8,128)} %gram.1) | data formatting | bytes 131072

commit v5 on v4

--- a/solution.py
+++ b/solution.py
@@ -17,11 +17,11 @@
 QT = B // 4
 EARLY, LATE = 528, 192
 ORDER = [(word[:1], int(word[1:])) for word in (
-    "l0", "z1", "z2", "t0", "y0", "w1", "w2", "z3", "z4", "t1", "y1", "t2", "s0", "y2", "w3", "w4", "z5", "z6",
-    "h0", "L0", "Z1", "Z2", "Z3", "Z4", "Z5", "Z6", "T0", "Y0", "t3", "s1", "y3", "t4", "s2", "y4", "z7", "Z7",
-    "S0", "T1", "Y1", "T2", "Y2", "p0", "s3", "S1", "p1", "S2", "p2", "T3", "Y3", "T4", "Y4", "x0", "t5", "y5",
-    "t6", "y6", "s4", "S3", "p3", "x1", "S4", "p4", "x2", "T5", "Y5", "T6", "Y6", "T7", "t7", "y7", "Y7", "s5",
-    "S5", "p5", "x3", "s6", "S6", "p6", "x4", "s7", "S7", "p7", "x5", "x6", "x7",
+    "l0", "z1", "z2", "t0", "y0", "w1", "z3", "w2", "z4", "t1", "y1", "t2", "s0", "y2", "h0", "L0", "Z1", "Z2",
+    "Z3", "Z4", "w3", "z5", "w4", "z6", "Z5", "Z6", "T0", "Y0", "t3", "s1", "y3", "t4", "s2", "y4", "z7", "Z7",
+    "S0", "T1", "Y1", "T2", "Y2", "p0", "s3", "S1", "p1", "S2", "p2", "T3", "Y3", "T4", "Y4", "T5", "Y5", "T6",
+    "Y6", "x0", "t5", "y5", "t6", "y6", "s4", "S3", "p3", "x1", "S4", "p4", "x2", "T7", "Y7", "t7", "y7", "s5",
+    "S5", "p5", "x3", "S6", "s6", "p6", "x4", "S7", "s7", "p7", "x5", "x6", "x7",
 )]
 
 

time: 94.1 us -> 88 us (0.935)
  Pallas kernels: 91.8 us -> 85.6 us
    pallas_call x1, Pallas kernels: 91.8 us -> 85.6 us  [shards(): pl.pallas_call(kernel, out_shape=jax.ShapeDtypeStruct((B, B), f32), in_sp...]
where the time goes in v5:
time: 88 us; the launch traced here: 87.1 us
  Pallas kernels  85.6 us (97%)
  local copies, waits for them, and re-layouts  1.47 us (2%)
    pallas_call x1, Pallas kernels, shards(): pl.pallas_call(kernel, out_shape=jax.ShapeDtypeStruct((B, B), f32), in_sp...  85.6 us

profile of v5, /device:TPU:33, one launch (start us, length us, event | category | flops | bytes accessed | tf_op | source)
XLA Modules:
  0.0 87.1 jit_solution(1999589555994108707)
XLA Ops:
  0.0 85.6 %gram.1 = f32[128,128]{1,0:T(8,128)} custom-call(bf16[8,720,128]{2,1,0:T(8,128)(2,1)} %bitcast.3, f32[2,4,720]{2,1,0:T(4,128)} %lon_ref.1, f32[2,4,720]{2,1,0:T(4,128)} %lat_ref.1, f32[64]{0:T(128)} %constant.2.clone.fac_ref), custom_call_target="tpu_custom_call" | custom-call | tf_op jit(solution)/shard_map/gram/pallas_call | solution.py:449
  85.6 1.5 %copy.6 = f32[128,128]{1,0:T(8,128)} copy(f32[128,128]{1,0:T(8,128)} %gram.1) | data formatting | bytes 131072

commit v6 on v5

--- a/solution.py
+++ b/solution.py
@@ -19,9 +19,10 @@
 ORDER = [(word[:1], int(word[1:])) for word in (
     "l0", "z1", "z2", "t0", "y0", "w1", "z3", "w2", "z4", "t1", "y1", "t2", "s0", "y2", "h0", "L0", "Z1", "Z2",
     "Z3", "Z4", "w3", "z5", "w4", "z6", "Z5", "Z6", "T0", "Y0", "t3", "s1", "y3", "t4", "s2", "y4", "z7", "Z7",
-    "S0", "T1", "Y1", "T2", "Y2", "p0", "s3", "S1", "p1", "S2", "p2", "T3", "Y3", "T4", "Y4", "T5", "Y5", "T6",
-    "Y6", "x0", "t5", "y5", "t6", "y6", "s4", "S3", "p3", "x1", "S4", "p4", "x2", "T7", "Y7", "t7", "y7", "s5",
-    "S5", "p5", "x3", "S6", "s6", "p6", "x4", "S7", "s7", "p7", "x5", "x6", "x7",
+    "S0", "T1", "Y1", "T2", "Y2", "q0", "p0", "s3", "S1", "q1", "p1", "S2", "q2", "p2", "T3", "Y3", "T4", "Y4",
+    "T5", "Y5", "T6", "Y6", "x0", "t5", "y5", "t6", "y6", "s4", "S3", "q3", "p3", "x1", "S4", "q4", "p4", "x2",
+    "T7", "Y7", "t7", "y7", "q5", "s5", "S5", "p5", "x3", "q6", "S6", "s6", "p6", "x4", "q7", "S7", "s7", "p7",
+    "x5", "x6", "x7",
 )]
 
 
@@ -258,7 +259,7 @@
         y_copy(1 - yl, near(n), late).wait_recv()
         c_copy(1 - yl, near(n), core, late).start()
 
-    def pairs(t, use, then):
+    def pairs(t, use, then, kinds="cr"):
         u = near(t)
 
         def each(n, what):
@@ -266,13 +267,15 @@
             k1 = (u + 8 - w - off) % 8
             k2 = (w + 8 - u - off) % 8
 
-            @pl.when(k1 < nb)
-            def _():
-                what(u, 4 - k1, w)
-
-            @pl.when((n < t) & (k2 < nb))
-            def _():
-                what(w, 4 - k2, u)
+            if "c" in kinds:
+                @pl.when(k1 < nb)
+                def _():
+                    what(u, 4 - k1, w)
+
+            if "r" in kinds:
+                @pl.when((n < t) & (k2 < nb))
+                def _():
+                    what(w, 4 - k2, u)
 
         def one(n, carry):
             each(n, use)
@@ -297,15 +300,18 @@
         x_all(m, kk).wait_recv()
         fin[m, kk] = part[m, quarter(kk, xx), :] + xin[m, kk, 0] + xin[m, kk, 1] + xin[m, kk, 2]
 
-    def products(t):
+    def row_products(t):
         turn(near(t))
+        pairs(t, multiply, send, "r")
+
+    def column_products(t):
         c_arrive(1 - yl, near(t))
-        pairs(t, multiply, send)
+        pairs(t, multiply, send, "c")
 
     def x_sum(t):
         pairs(t, add, f_start)
 
-    actions = {"h": rest_of_band, "p": products, "x": x_sum}
+    actions = {"h": rest_of_band, "q": row_products, "p": column_products, "x": x_sum}
     for late, names in enumerate(("lztysw", "LZTYSW")):
         for name, action in zip(names, (
                 lambda n, late: local_copy(late).start(),

time: 88 us -> 88.9 us (1.010)
  the two profiles are of different devices: /device:TPU:33 before, /device:TPU:39 now
where the time goes in v6:
time: 88.9 us; the launch traced here: 88.7 us
  Pallas kernels  87.2 us (98%)
  local copies, waits for them, and re-layouts  1.47 us (2%)
    pallas_call x1, Pallas kernels, shards(): pl.pallas_call(kernel, out_shape=jax.ShapeDtypeStruct((B, B), f32), in_sp...  87.2 us

profile of v6, /device:TPU:39, one launch (start us, length us, event | category | flops | bytes accessed | tf_op | source)
XLA Modules:
  0.0 88.7 jit_solution(1842652272000137195)
XLA Ops:
  0.0 87.2 %gram.1 = f32[128,128]{1,0:T(8,128)} custom-call(bf16[8,720,128]{2,1,0:T(8,128)(2,1)} %bitcast.3, f32[2,4,720]{2,1,0:T(4,128)} %lon_ref.1, f32[2,4,720]{2,1,0:T(4,128)} %lat_ref.1, f32[64]{0:T(128)} %constant.2.clone.fac_ref), custom_call_target="tpu_custom_call" | custom-call | tf_op jit(solution)/shard_map/gram/pallas_call | solution.py:455
  87.2 1.5 %copy.6 = f32[128,128]{1,0:T(8,128)} copy(f32[128,128]{1,0:T(8,128)} %gram.1) | data formatting | bytes 131072

commit v7 on v5

--- a/solution.py
+++ b/solution.py
@@ -17,9 +17,9 @@
 QT = B // 4
 EARLY, LATE = 528, 192
 ORDER = [(word[:1], int(word[1:])) for word in (
-    "l0", "z1", "z2", "t0", "y0", "w1", "z3", "w2", "z4", "t1", "y1", "t2", "s0", "y2", "h0", "L0", "Z1", "Z2",
-    "Z3", "Z4", "w3", "z5", "w4", "z6", "Z5", "Z6", "T0", "Y0", "t3", "s1", "y3", "t4", "s2", "y4", "z7", "Z7",
-    "S0", "T1", "Y1", "T2", "Y2", "p0", "s3", "S1", "p1", "S2", "p2", "T3", "Y3", "T4", "Y4", "T5", "Y5", "T6",
+    "l0", "z1", "z2", "t0", "y0", "w1", "z3", "w2", "z4", "t1", "y1", "t2", "y2", "s0", "h0", "L0", "Z1", "Z2",
+    "Z3", "Z4", "w3", "z5", "w4", "z6", "Z5", "Z6", "T0", "Y0", "T1", "Y1", "T2", "Y2", "t3", "s1", "y3", "t4",
+    "s2", "y4", "z7", "Z7", "S0", "p0", "S1", "p1", "S2", "p2", "T3", "Y3", "T4", "Y4", "s3", "T5", "Y5", "T6",
     "Y6", "x0", "t5", "y5", "t6", "y6", "s4", "S3", "p3", "x1", "S4", "p4", "x2", "T7", "Y7", "t7", "y7", "s5",
     "S5", "p5", "x3", "S6", "s6", "p6", "x4", "S7", "s7", "p7", "x5", "x6", "x7",
 )]

time: 88 us -> 88 us (level)
  no operation moved by 1% of the time
where the time goes in v7:
time: 88 us; the launch traced here: 86.8 us
  Pallas kernels  85.3 us (97%)
  local copies, waits for them, and re-layouts  1.47 us (2%)
    pallas_call x1, Pallas kernels, shards(): pl.pallas_call(kernel, out_shape=jax.ShapeDtypeStruct((B, B), f32), in_sp...  85.3 us

profile of v7, /device:TPU:33, one launch (start us, length us, event | category | flops | bytes accessed | tf_op | source)
XLA Modules:
  0.0 86.8 jit_solution(17297330670920358508)
XLA Ops:
  0.0 85.3 %gram.1 = f32[128,128]{1,0:T(8,128)} custom-call(bf16[8,720,128]{2,1,0:T(8,128)(2,1)} %bitcast.3, f32[2,4,720]{2,1,0:T(4,128)} %lon_ref.1, f32[2,4,720]{2,1,0:T(4,128)} %lat_ref.1, f32[64]{0:T(128)} %constant.2.clone.fac_ref), custom_call_target="tpu_custom_call" | custom-call | tf_op jit(solution)/shard_map/gram/pallas_call | solution.py:449
  85.3 1.5 %copy.6 = f32[128,128]{1,0:T(8,128)} copy(f32[128,128]{1,0:T(8,128)} %gram.1) | data formatting | bytes 131072

commit v8 on v5

--- a/solution.py
+++ b/solution.py
@@ -17,7 +17,7 @@
 QT = B // 4
 EARLY, LATE = 528, 192
 ORDER = [(word[:1], int(word[1:])) for word in (
-    "l0", "z1", "z2", "t0", "y0", "w1", "z3", "w2", "z4", "t1", "y1", "t2", "s0", "y2", "h0", "L0", "Z1", "Z2",
+    "l0", "z1", "z2", "t0", "y0", "w1", "z3", "w2", "z4", "h0", "L0", "Z1", "Z2", "t1", "y1", "t2", "s0", "y2",
     "Z3", "Z4", "w3", "z5", "w4", "z6", "Z5", "Z6", "T0", "Y0", "t3", "s1", "y3", "t4", "s2", "y4", "z7", "Z7",
     "S0", "T1", "Y1", "T2", "Y2", "p0", "s3", "S1", "p1", "S2", "p2", "T3", "Y3", "T4", "Y4", "T5", "Y5", "T6",
     "Y6", "x0", "t5", "y5", "t6", "y6", "s4", "S3", "p3", "x1", "S4", "p4", "x2", "T7", "Y7", "t7", "y7", "s5",

time: 88 us -> 88.1 us (level)
  no operation moved by 1% of the time
where the time goes in v8:
time: 88.1 us; the launch traced here: 86.6 us
  Pallas kernels  85.1 us (97%)
  local copies, waits for them, and re-layouts  1.47 us (2%)
    pallas_call x1, Pallas kernels, shards(): pl.pallas_call(kernel, out_shape=jax.ShapeDtypeStruct((B, B), f32), in_sp...  85.1 us

profile of v8, /device:TPU:33, one launch (start us, length us, event | category | flops | bytes accessed | tf_op | source)
XLA Modules:
  0.0 86.6 jit_solution(1442555914133688319)
XLA Ops:
  0.0 85.1 %gram.1 = f32[128,128]{1,0:T(8,128)} custom-call(bf16[8,720,128]{2,1,0:T(8,128)(2,1)} %bitcast.3, f32[2,4,720]{2,1,0:T(4,128)} %lon_ref.1, f32[2,4,720]{2,1,0:T(4,128)} %lat_ref.1, f32[64]{0:T(128)} %constant.2.clone.fac_ref), custom_call_target="tpu_custom_call" | custom-call | tf_op jit(solution)/shard_map/gram/pallas_call | solution.py:449
  85.1 1.5 %copy.6 = f32[128,128]{1,0:T(8,128)} copy(f32[128,128]{1,0:T(8,128)} %gram.1) | data formatting | bytes 131072
